TPU v7x, 32 devices: a whole 2x2x4 slice. The times are simulated.
32 devices in a mesh: row: 8 (over z, y), col: 4 (over x, core).
Axes of the slice: x: 2, y: 2, z: 4, core: 2. Of those that a mesh axis runs over, the one named last changes fastest.
Arguments:
- basis_values: bfloat16 [4, 4096, 4096], P(None, 'row', 'col'), may hold values from -6 to 6
- density: float32 [4096, 2560], P('row'), may hold values from -1 to 1, as said below
- screen: int32 [32, 32], P('row', 'col'), may hold values 0 or 1
- atom_of_block: int32 [32], P('col'), may hold values from 0 to 63
- atom_factor: float32 [64], replicated, may hold values from 0.5 to 2
- quad_weight: float32 [4096], P('col'), may hold values from 0.5 to 2
- core_density: float32 [4096], P('col'), may hold values from 0.3 to 1
Outputs:
- xc_matrix: float32 [4096, 1536], P(('row', 'col'))
Inputs may be any that keep to these rules, and one draw needn't show every extreme that they name: The density matrix is symmetric. Column block k of a row (k from 0 to 4, 512 columns each) holds the row's entries with the basis block k - 2 places further along the closed chain of 8 blocks; all other entries are zero.
All inputs are finite; a program needn't handle non-finite values. No bound on the sum of `screen` on one device may be relied on, other than what follows from the above.
Results may differ from a plain program's by a relative error of at most 0.0014.
Values may be sent and summed in bfloat16 or wider, within the bound.
No kernel may reach another device: no remote copies, remote signals or barrier semaphores. Data moves between devices by JAX's collectives and lax.ppermute only.
A program may use at most 64 MiB of HBM per device.

v0:
```python
import math
import jax
import jax.numpy as jnp
from jax import lax
from jax.sharding import PartitionSpec as P

BAND = 5
KAPPA_VALUE = 0.804
MU_VALUE = 0.22
SLATER_COEF = 0.7386


def from_behind(block, axis, distance):
    devices = range(lax.axis_size(axis))
    route = [((i - distance) % len(devices), i) for i in devices]
    return lax.ppermute(block, axis, route)


def energy_density(density_in, squared_in, core):
    regular = jnp.sqrt(density_in * density_in + core * core)
    reduced = squared_in * regular ** (-8.0 / 3.0)
    enhance = 1.0 + KAPPA_VALUE - KAPPA_VALUE / (1.0 + MU_VALUE * reduced / KAPPA_VALUE)
    return -SLATER_COEF * regular ** (4.0 / 3.0) * enhance


def potentials(density_in, squared_in, core):

    def total_energy(first_arg, second_arg):
        return jnp.sum(energy_density(first_arg, second_arg, core))

    return jax.grad(total_energy, argnums=(0, 1))(density_in, squared_in)


def masked_basis(basis_values, screen):
    components, row_count, points = basis_values.shape
    row_blocks, point_blocks = screen.shape
    shaped = basis_values.reshape(
        components, row_blocks, row_count // row_blocks, point_blocks, points // point_blocks
    )
    keeper = screen.astype(basis_values.dtype)[None, :, None, :, None]
    return (shaped * keeper).reshape(components, row_count, points)


def contract(left_side, right_side):
    return lax.dot_general(
        left_side, right_side, (((1,), (1,)), ((), ())), preferred_element_type=jnp.float32
    )


def body(basis_values, density, screen, atom_of_block, atom_factor, quad_weight, core_density):
    masked = masked_basis(basis_values, screen)
    values = masked[0]
    row_count, points = values.shape
    reach = BAND // 2
    nearby = {0: values}
    for heading in (1, -1):
        current = values
        for stride in range(1, reach + 1):
            current = from_behind(current, "row", -heading)
            nearby[heading * stride] = current
    applied = jnp.zeros((row_count, points), jnp.float32)
    for offset in range(-reach, reach + 1):
        column = offset + reach
        strip = density[:, column * row_count : (column + 1) * row_count]
        applied = applied + jnp.dot(
            strip, nearby[offset].astype(jnp.float32), precision=lax.Precision.HIGHEST
        )
    masked32 = masked.astype(jnp.float32)
    partial_sums = jnp.einsum("cmg,mg->cg", masked32, applied, precision=lax.Precision.HIGHEST)
    summed = lax.psum(partial_sums, "row")
    point_density = summed[0]
    gradient = 2.0 * summed[1:]
    squared = jnp.sum(gradient * gradient, axis=0)
    atoms = atom_factor.shape[0]
    chooser = (atom_of_block[:, None] == jnp.arange(atoms, dtype=jnp.int32)[None, :]).astype(
        jnp.float32
    )
    block_factor = jnp.dot(chooser, atom_factor, precision=lax.Precision.HIGHEST)
    group_size = points // atom_of_block.shape[0]
    weights = (quad_weight.reshape(-1, group_size) * block_factor[:, None]).reshape(
        points
    ) / math.sqrt(points * lax.axis_size("col"))
    density_pot, gradient_pot = potentials(point_density, squared, core_density)
    scalar_part = 0.5 * weights * density_pot
    vector_part = 2.0 * weights * gradient_pot * gradient
    half_pot = (
        scalar_part * masked32[0] + jnp.sum(vector_part[:, None, :] * masked32[1:], axis=0)
    ).astype(jnp.bfloat16)
    pieces = [contract(half_pot, values) + contract(values, half_pot)]
    for local_offset in range(1, reach + 1):
        pieces.append(contract(half_pot, nearby[local_offset]))
    for local_offset in range(1, reach + 1):
        lower_rows = nearby[-local_offset]
        pieces.append(contract(lower_rows, half_pot))
    summed_terms = lax.psum_scatter(
        jnp.concatenate(pieces, axis=1), "col", scatter_dimension=0, tiled=True
    )
    result = [summed_terms[:, :row_count]]
    for offset in range(1, reach + 1):
        start_col = (reach + offset) * row_count
        mirrored = from_behind(
            summed_terms[:, start_col : start_col + row_count].astype(jnp.bfloat16), "row", -offset
        ).astype(jnp.float32)
        result.append(summed_terms[:, offset * row_count : (offset + 1) * row_count] + mirrored)
    return jnp.concatenate(result, axis=1)


def solution(mesh):
    in_specs = (
        P(None, "row", "col"),
        P("row", None),
        P("row", "col"),
        P("col"),
        P(),
        P("col"),
        P("col"),
    )
    out_specs = P(("row", "col"), None)
    return jax.shard_map(body, mesh=mesh, in_specs=in_specs, out_specs=out_specs, check_vma=False)
```

profile of v0, /device:TPU:0, one launch (start us, length us, event | category | flops | bytes accessed | tf_op | source)
XLA Modules:
  0.0 244.4 jit_solution(6484854692076097885)
XLA Ops:
  6.5 0.0 copy-start
  6.5 0.0 reduce-scatter.2.cloned.1.call-start
  6.5 0.7 convert_element_type.29
  7.2 3.3 %copy.18 = bf16[256,8,8,128]{3,2,1,0:T(8,128)(2,1)S(1)} copy(bf16[256,8,8,128]{3,1,2,0:T(8,128)(2,1)} %bitcast.64) | data formatting | bytes 8388608
  10.5 0.0 copy-start.1
  10.5 0.1 slice_multiply_fusion.1
  10.7 0.3 copy.27
  10.9 3.0 %collective-permute-start = (bf16[512,1024]{1,0:T(8,128)(2,1)S(1)}, bf16[512,1024]{1,0:T(8,128)(2,1)S(1)}, u32[]{:S(2)}, u32[]{:S(2)}) collective-permute-start(bf16[512,1024]{1,0:T(8,128)(2,1)S(1)} %bitcast.75), channel_id=1, source_target_pairs={{28,0},{0,4},{4,8},{8,12},{12,16},{16,20},{20,24},{24,28},{29,1},{... | collective-permute-start | bytes 3145736 | tf_op jit(solution)/shard_map/ppermute | solution.py:16
  14.0 3.1 %collective-permute-start.2 = (bf16[512,1024]{1,0:T(8,128)(2,1)S(1)}, bf16[512,1024]{1,0:T(8,128)(2,1)S(1)}, u32[]{:S(2)}, u32[]{:S(2)}) collective-permute-start(bf16[512,1024]{1,0:T(8,128)(2,1)S(1)} %bitcast.76), channel_id=1, source_target_pairs={{4,0},{8,4},{12,8},{16,12},{20,16},{24,20},{28,24},{0,28},{5,1},{9... | collective-permute-start | bytes 3145736 | tf_op jit(solution)/shard_map/ppermute | solution.py:16
  17.1 0.2 mul.148
  17.3 0.0 slice-start
  17.3 0.3 copy.26
  17.6 0.0 copy-done.1
  17.6 0.0 slice-start.1
  17.6 4.2 %multiply_convert_fusion = f32[4,512,1024]{2,1,0:T(8,128)} fusion(bf16[4,512,1024]{2,1,0:T(8,128)(2,1)S(1)} %copy-done.1, bf16[512,1024]{1,0:T(8,128)(2,1)S(1)} %bitcast.69), kind=kLoop, calls=%fused_computation.3 | loop fusion | flops 4194304 | bytes 13631488 | tf_op jit(solution)/shard_map/convert_element_type | solution.py:68
  21.8 37.1 %collective-permute-done = bf16[512,1024]{1,0:T(8,128)(2,1)S(1)} collective-permute-done((bf16[512,1024]{1,0:T(8,128)(2,1)S(1)}, bf16[512,1024]{1,0:T(8,128)(2,1)S(1)}, u32[]{:S(2)}, u32[]{:S(2)}) %collective-permute-start) | collective-permute-done | bytes 1048608 | tf_op jit(solution)/shard_map/ppermute | solution.py:16
  58.9 2.5 %collective-permute-start.1 = (bf16[512,1024]{1,0:T(8,128)(2,1)S(1)}, bf16[512,1024]{1,0:T(8,128)(2,1)S(1)}, u32[]{:S(2)}, u32[]{:S(2)}) collective-permute-start(bf16[512,1024]{1,0:T(8,128)(2,1)S(1)} %collective-permute-done), channel_id=1, source_target_pairs={{28,0},{0,4},{4,8},{8,12},{12,16},{16,20},{20,24},{24,28},{29,1},{... | collective-permute-start | bytes 3145736 | tf_op jit(solution)/shard_map/ppermute | solution.py:16
  61.4 0.0 slice-done
  61.4 0.0 slice-done.1
  61.4 2.2 fusion.9
  63.6 0.0 collective-permute-done.2
  63.6 0.0 copy-start.4
  63.6 3.3 %collective-permute-start.3 = (bf16[512,1024]{1,0:T(8,128)(2,1)S(1)}, bf16[512,1024]{1,0:T(8,128)(2,1)S(1)}, u32[]{:S(2)}, u32[]{:S(2)}) collective-permute-start(bf16[512,1024]{1,0:T(8,128)(2,1)S(1)} %collective-permute-done.2), channel_id=1, source_target_pairs={{4,0},{8,4},{12,8},{16,12},{20,16},{24,20},{28,24},{0,28},{5,1},{9... | collective-permute-start | bytes 3145736 | tf_op jit(solution)/shard_map/ppermute | solution.py:16
  66.9 0.0 copy-done
  66.9 0.0 copy-done.10
  66.9 0.2 convolution_bitcast_fusion
  67.1 2.2 fusion.11
  69.3 0.0 copy-done.2
  69.3 2.2 fusion.7
  71.5 0.0 copy-done.4
  71.5 33.9 %collective-permute-done.1 = bf16[512,1024]{1,0:T(8,128)(2,1)S(1)} collective-permute-done((bf16[512,1024]{1,0:T(8,128)(2,1)S(1)}, bf16[512,1024]{1,0:T(8,128)(2,1)S(1)}, u32[]{:S(2)}, u32[]{:S(2)}) %collective-permute-start.1) | collective-permute-done | bytes 1048608 | tf_op jit(solution)/shard_map/ppermute | solution.py:16
  105.4 1.1 copy-done.6
  106.5 2.2 fusion.13
  108.7 0.5 collective-permute-done.3
  109.2 3.9 %add_add_fusion = f32[1024,512]{1,0:T(8,128)} fusion(f32[1024,512]{1,0:T(8,128)S(1)} %fusion.7, f32[1024,512]{1,0:T(8,128)S(1)} %fusion.9, f32[1024,512]{1,0:T(8,128)S(1)} %fusion.13, f32[1024,512]{1,0:T(8,128)S(1)} %fusion.11, bf16[512,1024]{1,0:T(8,128)(2,1)S(1)} %collective-permute-done.3, f32[512,2560]{1,0:T(8,128)S(1)} %bitcast.73), kind=kOutput, calls=%fused_computation.9 | convolution fusion | flops 3223322624 | bytes 12582912 | tf_op jit(solution)/shard_map/dot_general | solution.py:65
  113.1 2.9 %copy.16 = f32[1024,512]{0,1:T(8,128)} copy(f32[1024,512]{1,0:T(8,128)} %add_add_fusion) | data formatting | bytes 4194304
  116.0 4.3 %multiply_reduce_fusion = f32[1024,4]{0,1:T(4,128)S(1)} fusion(f32[1024,512]{0,1:T(8,128)} %copy.16, bf16[4,512,1024]{2,1,0:T(8,128)(2,1)} %param.7, bf16[512,1024]{1,0:T(8,128)(2,1)S(1)} %bitcast.70), kind=kLoop, calls=%fused_computation | loop fusion | flops 8384512 | bytes 7356416 | tf_op jit(solution)/shard_map/cmg,mg->cg/dot_general | solution.py:69
  120.3 37.9 %psum.7 = f32[4,1024]{1,0:T(4,128)S(1)} all-reduce(f32[4,1024]{1,0:T(4,128)S(1)} %bitcast.77), channel_id=1, replica_groups=mesh['row'=8,'col'=4] {'row'}, use_global_device_ids=true, to_apply=%region_0.0 | all-reduce | flops 4096 | bytes 32768 | tf_op jit(solution)/shard_map/psum | solution.py:70
  158.2 0.0 copy-done.8
  158.2 0.0 copy-done.9
  158.2 0.1 multiply_multiply_fusion
  158.3 3.9 %fusion = f32[512,1024]{1,0:T(8,128)S(1)} fusion(f32[4,512,1024]{2,1,0:T(8,128)} %multiply_convert_fusion, f32[3,1024]{1,0:T(4,128)S(1)} %slice_multiply_fusion.2), kind=kLoop, calls=%fused_computation.2 | loop fusion | flops 2621440 | bytes 8400896 | tf_op jit(solution)/shard_map/reduce_sum | solution.py:87
  162.3 1.9 fusion.2
  164.2 1.9 fusion.5
  166.1 0.0 copy-start.5
  166.1 0.8 fusion.17
  166.8 1.7 fusion.4
  168.6 0.0 copy-done.5
  168.6 1.7 convolution_dynamic-update-slice_fusion.3
  170.3 1.7 convolution_dynamic-update-slice_fusion.2
  172.0 0.0 copy-done.3
  172.0 1.8 convolution_dynamic-update-slice_fusion.1
  173.8 0.0 copy-done.7
  173.8 1.7 convolution_dynamic-update-slice_fusion
  175.5 0.0 reduce-scatter.2.cloned.1.call-update
  175.5 48.5 %reduce-scatter.2.cloned.1.call-done = f32[128,2560]{0,1:T(8,128)} async-done(((f32[512,2560]{0,1:T(8,128)}), f32[128,2560]{0,1:T(8,128)}) %reduce-scatter.2.cloned.1.call-update) | async-done | bytes 1310736 | tf_op jit(solution)/shard_map/reduce_scatter | solution.py:95
  224.1 1.4 convert.4
  225.5 4.3 %collective-permute-start.4 = (bf16[128,512]{0,1:T(8,128)(2,1)S(1)}, bf16[128,512]{0,1:T(8,128)(2,1)S(1)}, u32[]{:S(2)}, u32[]{:S(2)}) collective-permute-start(bf16[128,512]{0,1:T(8,128)(2,1)S(1)} %get-tuple-element.8), channel_id=1, source_target_pairs={{4,0},{8,4},{12,8},{16,12},{20,16},{24,20},{28,24},{0,28},{5,1},{9... | collective-permute-start | bytes 393224 | tf_op jit(solution)/shard_map/ppermute | solution.py:16
  229.8 0.5 collective-permute-start.5
  230.3 3.4 %collective-permute-done.4 = bf16[128,512]{0,1:T(8,128)(2,1)S(1)} collective-permute-done((bf16[128,512]{0,1:T(8,128)(2,1)S(1)}, bf16[128,512]{0,1:T(8,128)(2,1)S(1)}, u32[]{:S(2)}, u32[]{:S(2)}) %collective-permute-start.4) | collective-permute-done | bytes 131104 | tf_op jit(solution)/shard_map/ppermute | solution.py:16
  233.7 1.5 collective-permute-done.5
  235.2 1.2 fusion.18
  236.4 0.1 pad_maximum_fusion
  236.4 1.1 copy.8
  (12 shorter events, 0.1 us)
Async XLA Ops:
  6.5 60.4 %copy-start = (f32[64]{0:T(128)S(1)}, f32[64]{0:T(128)}, u32[]{:S(2)}) copy-start(f32[64]{0:T(128)} %param.11) | copy-start | bytes 772
  6.5 217.5 %reduce-scatter.2.cloned.1.call-start = ((), (), s32[]{:S(2)}) async-start(), calls=%async_computation.1 | async-start | bytes 6553600 | tf_op jit(solution)/shard_map/reduce_scatter | solution.py:95
  10.5 7.1 %copy-start.1 = (bf16[4,512,1024]{2,1,0:T(8,128)(2,1)S(1)}, bf16[4,512,1024]{2,1,0:T(8,128)(2,1)}, u32[]{:S(2)}) copy-start(bf16[4,512,1024]{2,1,0:T(8,128)(2,1)} %param.7) | copy-start | bytes 12582916
  10.9 47.9 %collective-permute-start = (bf16[512,1024]{1,0:T(8,128)(2,1)S(1)}, bf16[512,1024]{1,0:T(8,128)(2,1)S(1)}, u32[]{:S(2)}, u32[]{:S(2)}) collective-permute-start(bf16[512,1024]{1,0:T(8,128)(2,1)S(1)} %bitcast.75), channel_id=1, source_target_pairs={{28,0},{0,4},{4,8},{8,12},{12,16},{16,20},{20,24},{24,28},{29,1},{... | collective-permute-start | bytes 3145736 | tf_op jit(solution)/shard_map/ppermute | solution.py:16
  14.0 49.6 %collective-permute-start.2 = (bf16[512,1024]{1,0:T(8,128)(2,1)S(1)}, bf16[512,1024]{1,0:T(8,128)(2,1)S(1)}, u32[]{:S(2)}, u32[]{:S(2)}) collective-permute-start(bf16[512,1024]{1,0:T(8,128)(2,1)S(1)} %bitcast.76), channel_id=1, source_target_pairs={{4,0},{8,4},{12,8},{16,12},{20,16},{24,20},{28,24},{0,28},{5,1},{9... | collective-permute-start | bytes 3145736 | tf_op jit(solution)/shard_map/ppermute | solution.py:16
  17.3 44.1 %slice-start = ((s8[5242880]{0:T(1024)(128)(4,1)}), s8[4194304]{0:T(1024)(128)(4,1)S(1)}, s32[]{:S(2)}) async-start(s8[5242880]{0:T(1024)(128)(4,1)} %bitcast.72), calls=%async_computation.2 | async-start | bytes 8388608
  17.6 43.8 %slice-start.1 = ((s8[5242880]{0:T(1024)(128)(4,1)}), s8[1048576]{0:T(1024)(128)(4,1)S(1)}, s32[]{:S(2)}) async-start(s8[5242880]{0:T(1024)(128)(4,1)} %bitcast.72), calls=%async_computation.3 | async-start | bytes 2097152
  21.8 45.1 %copy-start.10 = (s32[8]{0:T(128)S(1)}, s32[8]{0:T(128)}, u32[]{:S(2)}) copy-start(s32[8]{0:T(128)} %param.10) | copy-start | bytes 100
  58.9 10.4 %copy-start.2 = (bf16[512,1024]{1,0:T(8,128)(2,1)}, bf16[512,1024]{1,0:T(8,128)(2,1)S(1)}, u32[]{:S(2)}) copy-start(bf16[512,1024]{1,0:T(8,128)(2,1)S(1)} %collective-permute-done) | copy-start | bytes 3145732
  58.9 46.5 %collective-permute-start.1 = (bf16[512,1024]{1,0:T(8,128)(2,1)S(1)}, bf16[512,1024]{1,0:T(8,128)(2,1)S(1)}, u32[]{:S(2)}, u32[]{:S(2)}) collective-permute-start(bf16[512,1024]{1,0:T(8,128)(2,1)S(1)} %collective-permute-done), channel_id=1, source_target_pairs={{28,0},{0,4},{4,8},{8,12},{12,16},{16,20},{20,24},{24,28},{29,1},{... | collective-permute-start | bytes 3145736 | tf_op jit(solution)/shard_map/ppermute | solution.py:16
  63.6 7.9 %copy-start.4 = (bf16[512,1024]{1,0:T(8,128)(2,1)}, bf16[512,1024]{1,0:T(8,128)(2,1)S(1)}, u32[]{:S(2)}) copy-start(bf16[512,1024]{1,0:T(8,128)(2,1)S(1)} %collective-permute-done.2) | copy-start | bytes 3145732
  63.6 45.6 %collective-permute-start.3 = (bf16[512,1024]{1,0:T(8,128)(2,1)S(1)}, bf16[512,1024]{1,0:T(8,128)(2,1)S(1)}, u32[]{:S(2)}, u32[]{:S(2)}) collective-permute-start(bf16[512,1024]{1,0:T(8,128)(2,1)S(1)} %collective-permute-done.2), channel_id=1, source_target_pairs={{4,0},{8,4},{12,8},{16,12},{20,16},{24,20},{28,24},{0,28},{5,1},{9... | collective-permute-start | bytes 3145736 | tf_op jit(solution)/shard_map/ppermute | solution.py:16
  105.4 1.1 copy-start.6
  116.0 42.2 %copy-start.8 = (f32[1024]{0:T(1024)S(1)}, f32[1024]{0:T(1024)}, u32[]{:S(2)}) copy-start(f32[1024]{0:T(1024)} %param.12) | copy-start | bytes 12292
  116.0 42.2 %copy-start.9 = (f32[1024]{0:T(1024)S(1)}, f32[1024]{0:T(1024)}, u32[]{:S(2)}) copy-start(f32[1024]{0:T(1024)} %param.13) | copy-start | bytes 12292
  166.1 2.5 %copy-start.5 = (bf16[512,1024]{1,0:T(8,128)(2,1)S(1)}, bf16[512,1024]{1,0:T(8,128)(2,1)}, u32[]{:S(2)}) copy-start(bf16[512,1024]{1,0:T(8,128)(2,1)} %copy-done.4) | copy-start | bytes 3145732
  168.6 3.5 %copy-start.3 = (bf16[512,1024]{1,0:T(8,128)(2,1)S(1)}, bf16[512,1024]{1,0:T(8,128)(2,1)}, u32[]{:S(2)}) copy-start(bf16[512,1024]{1,0:T(8,128)(2,1)} %copy-done.2) | copy-start | bytes 3145732
  170.3 3.5 %copy-start.7 = (bf16[512,1024]{1,0:T(8,128)(2,1)S(1)}, bf16[512,1024]{1,0:T(8,128)(2,1)}, u32[]{:S(2)}) copy-start(bf16[512,1024]{1,0:T(8,128)(2,1)} %copy-done.6) | copy-start | bytes 3145732
  225.5 8.2 %collective-permute-start.4 = (bf16[128,512]{0,1:T(8,128)(2,1)S(1)}, bf16[128,512]{0,1:T(8,128)(2,1)S(1)}, u32[]{:S(2)}, u32[]{:S(2)}) collective-permute-start(bf16[128,512]{0,1:T(8,128)(2,1)S(1)} %get-tuple-element.8), channel_id=1, source_target_pairs={{4,0},{8,4},{12,8},{16,12},{20,16},{24,20},{28,24},{0,28},{5,1},{9... | collective-permute-start | bytes 393224 | tf_op jit(solution)/shard_map/ppermute | solution.py:16
  229.8 5.4 %collective-permute-start.5 = (bf16[128,512]{0,1:T(8,128)(2,1)S(1)}, bf16[128,512]{0,1:T(8,128)(2,1)S(1)}, u32[]{:S(2)}, u32[]{:S(2)}) collective-permute-start(bf16[128,512]{0,1:T(8,128)(2,1)S(1)} %get-tuple-element.9), channel_id=1, source_target_pairs={{8,0},{12,4},{16,8},{20,12},{24,16},{28,20},{0,24},{4,28},{9,1},{1... | collective-permute-start | bytes 393224 | tf_op jit(solution)/shard_map/ppermute | solution.py:16
Sparse Core Ops, SparseCore 0:
  175.6 48.3 reduce-scatter.1
where the time goes:
time: 245 us; the launch traced here: 244 us
  waiting for transfers between devices  125 us (51%)
  blocking collectives  37.9 us (15%)
  matrix products  22.3 us (9%)
  other arithmetic  19.8 us (8%)
  starting transfers between devices  16.8 us (7%)
  between operations  13.6 us (6%)
  local copies, waits for them, and re-layouts  9.21 us (4%)
    ppermute x6, waiting for transfers between devices, from_behind(): return lax.ppermute(block, axis, route)  76.3 us
    reduce_scatter x1, waiting for transfers between devices, body(): lax.psum_scatter(jnp.concatenate(pieces, axis=1), 'col', scatter_dimensio...  48.5 us
    psum x1, blocking collectives, body(): summed = lax.psum(partial_sums, 'row')  37.9 us
    ppermute x6, starting transfers between devices, from_behind(): return lax.ppermute(block, axis, route)  16.8 us
    dot_general x5, matrix products, body(): jnp.dot(strip, nearby[offset].astype(jnp.float32), precision=lax.Precisio...  12.7 us
    dot_general x6, matrix products, contract(): lax.dot_general(left_side, right_side, (((1,), (1,)), ((), ())), preferre...  9.41 us
    unnamed x30, local copies, waits for them, and re-layouts  7.84 us
  transfers between devices with their start and end apart: 7, of which 6 were waited for; matrix products, arithmetic and copies ran while one was open for 6% of the time, Pallas kernels for 0%

commit v1 on v0

--- a/solution.py
+++ b/solution.py
@@ -67,7 +67,8 @@
         )
     masked32 = masked.astype(jnp.float32)
     partial_sums = jnp.einsum("cmg,mg->cg", masked32, applied, precision=lax.Precision.HIGHEST)
-    summed = lax.psum(partial_sums, "row")
+    parts = lax.all_gather(partial_sums, "row", axis=0, tiled=False)
+    summed = parts.sum(axis=0)
     point_density = summed[0]
     gradient = 2.0 * summed[1:]
     squared = jnp.sum(gradient * gradient, axis=0)

time: 245 us -> 242 us (0.988)
  blocking collectives: 37.9 us -> 31.1 us
  waiting for transfers between devices: 125 us -> 129 us
    psum x1 -> x0, blocking collectives: 37.9 us -> none  [body(): summed = lax.psum(partial_sums, 'row')]
    all_gather x0 -> x1, blocking collectives: none -> 31.1 us  [body(): parts = lax.all_gather(partial_sums, 'row', axis=0, tiled=False)]
    reduce_scatter x1, waiting for transfers between devices: 48.5 us -> 52.7 us  [body(): lax.psum_scatter(jnp.concatenate(pieces, axis=1), 'col', scatter_dimensio...]
where the time goes in v1:
time: 242 us
  waiting for transfers between devices  129 us (53%)
  blocking collectives  31.1 us (13%)
  matrix products  22.3 us (9%)
  other arithmetic  19.8 us (8%)
  starting transfers between devices  16.8 us (7%)
  between operations  13.6 us (6%)
  local copies, waits for them, and re-layouts  9.21 us (4%)
    ppermute x6, waiting for transfers between devices, from_behind(): return lax.ppermute(block, axis, route)  76.3 us
    reduce_scatter x1, waiting for transfers between devices, body(): lax.psum_scatter(jnp.concatenate(pieces, axis=1), 'col', scatter_dimensio...  52.7 us
    all_gather x1, blocking collectives, body(): parts = lax.all_gather(partial_sums, 'row', axis=0, tiled=False)  31.1 us
    ppermute x6, starting transfers between devices, from_behind(): return lax.ppermute(block, axis, route)  16.8 us
    dot_general x5, matrix products, body(): jnp.dot(strip, nearby[offset].astype(jnp.float32), precision=lax.Precisio...  12.7 us
    dot_general x6, matrix products, contract(): lax.dot_general(left_side, right_side, (((1,), (1,)), ((), ())), preferre...  9.4 us
    unnamed x30, local copies, waits for them, and re-layouts  7.84 us
  transfers between devices with their start and end apart: 7, of which 6 were waited for; matrix products, arithmetic and copies ran while one was open for 6% of the time, Pallas kernels for 0%

profile of v1, /device:TPU:0, one launch (start us, length us, event | category | flops | bytes accessed | tf_op | source)
XLA Modules:
  0.0 241.8 jit_solution(17568296601416926260)
XLA Ops:
  6.5 0.0 copy-start
  6.5 0.0 reduce-scatter.2.cloned.1.call-start
  6.5 0.7 convert_element_type.29
  7.2 3.3 %copy.19 = bf16[256,8,8,128]{3,2,1,0:T(8,128)(2,1)S(1)} copy(bf16[256,8,8,128]{3,1,2,0:T(8,128)(2,1)} %bitcast.66) | data formatting | bytes 8388608
  10.5 0.0 copy-start.1
  10.5 0.1 slice_multiply_fusion.1
  10.7 0.3 copy.28
  10.9 3.0 %collective-permute-start = (bf16[512,1024]{1,0:T(8,128)(2,1)S(1)}, bf16[512,1024]{1,0:T(8,128)(2,1)S(1)}, u32[]{:S(2)}, u32[]{:S(2)}) collective-permute-start(bf16[512,1024]{1,0:T(8,128)(2,1)S(1)} %bitcast.77), channel_id=1, source_target_pairs={{28,0},{0,4},{4,8},{8,12},{12,16},{16,20},{20,24},{24,28},{29,1},{... | collective-permute-start | bytes 3145736 | tf_op jit(solution)/shard_map/ppermute | solution.py:16
  14.0 3.1 %collective-permute-start.2 = (bf16[512,1024]{1,0:T(8,128)(2,1)S(1)}, bf16[512,1024]{1,0:T(8,128)(2,1)S(1)}, u32[]{:S(2)}, u32[]{:S(2)}) collective-permute-start(bf16[512,1024]{1,0:T(8,128)(2,1)S(1)} %bitcast.78), channel_id=1, source_target_pairs={{4,0},{8,4},{12,8},{16,12},{20,16},{24,20},{28,24},{0,28},{5,1},{9... | collective-permute-start | bytes 3145736 | tf_op jit(solution)/shard_map/ppermute | solution.py:16
  17.1 0.2 mul.148
  17.3 0.0 slice-start
  17.3 0.3 copy.27
  17.6 0.0 copy-done.1
  17.6 0.0 slice-start.1
  17.6 4.2 %multiply_convert_fusion = f32[4,512,1024]{2,1,0:T(8,128)} fusion(bf16[4,512,1024]{2,1,0:T(8,128)(2,1)S(1)} %copy-done.1, bf16[512,1024]{1,0:T(8,128)(2,1)S(1)} %bitcast.71), kind=kLoop, calls=%fused_computation.3 | loop fusion | flops 4194304 | bytes 13631488 | tf_op jit(solution)/shard_map/convert_element_type | solution.py:68
  21.8 37.1 %collective-permute-done = bf16[512,1024]{1,0:T(8,128)(2,1)S(1)} collective-permute-done((bf16[512,1024]{1,0:T(8,128)(2,1)S(1)}, bf16[512,1024]{1,0:T(8,128)(2,1)S(1)}, u32[]{:S(2)}, u32[]{:S(2)}) %collective-permute-start) | collective-permute-done | bytes 1048608 | tf_op jit(solution)/shard_map/ppermute | solution.py:16
  58.9 2.5 %collective-permute-start.1 = (bf16[512,1024]{1,0:T(8,128)(2,1)S(1)}, bf16[512,1024]{1,0:T(8,128)(2,1)S(1)}, u32[]{:S(2)}, u32[]{:S(2)}) collective-permute-start(bf16[512,1024]{1,0:T(8,128)(2,1)S(1)} %collective-permute-done), channel_id=1, source_target_pairs={{28,0},{0,4},{4,8},{8,12},{12,16},{16,20},{20,24},{24,28},{29,1},{... | collective-permute-start | bytes 3145736 | tf_op jit(solution)/shard_map/ppermute | solution.py:16
  61.4 0.0 slice-done
  61.4 0.0 slice-done.1
  61.4 2.2 fusion.9
  63.6 0.0 collective-permute-done.2
  63.6 0.0 copy-start.4
  63.6 3.3 %collective-permute-start.3 = (bf16[512,1024]{1,0:T(8,128)(2,1)S(1)}, bf16[512,1024]{1,0:T(8,128)(2,1)S(1)}, u32[]{:S(2)}, u32[]{:S(2)}) collective-permute-start(bf16[512,1024]{1,0:T(8,128)(2,1)S(1)} %collective-permute-done.2), channel_id=1, source_target_pairs={{4,0},{8,4},{12,8},{16,12},{20,16},{24,20},{28,24},{0,28},{5,1},{9... | collective-permute-start | bytes 3145736 | tf_op jit(solution)/shard_map/ppermute | solution.py:16
  66.9 0.0 copy-done
  66.9 0.0 copy-done.10
  66.9 0.2 convolution_bitcast_fusion
  67.1 2.2 fusion.11
  69.3 0.0 copy-done.2
  69.3 2.2 fusion.7
  71.5 0.0 copy-done.4
  71.5 33.9 %collective-permute-done.1 = bf16[512,1024]{1,0:T(8,128)(2,1)S(1)} collective-permute-done((bf16[512,1024]{1,0:T(8,128)(2,1)S(1)}, bf16[512,1024]{1,0:T(8,128)(2,1)S(1)}, u32[]{:S(2)}, u32[]{:S(2)}) %collective-permute-start.1) | collective-permute-done | bytes 1048608 | tf_op jit(solution)/shard_map/ppermute | solution.py:16
  105.4 1.1 copy-done.6
  106.5 2.2 fusion.13
  108.7 0.5 collective-permute-done.3
  109.2 3.9 %add_add_fusion = f32[1024,512]{1,0:T(8,128)} fusion(f32[1024,512]{1,0:T(8,128)S(1)} %fusion.7, f32[1024,512]{1,0:T(8,128)S(1)} %fusion.9, f32[1024,512]{1,0:T(8,128)S(1)} %fusion.13, f32[1024,512]{1,0:T(8,128)S(1)} %fusion.11, bf16[512,1024]{1,0:T(8,128)(2,1)S(1)} %collective-permute-done.3, f32[512,2560]{1,0:T(8,128)S(1)} %bitcast.75), kind=kOutput, calls=%fused_computation.9 | convolution fusion | flops 3223322624 | bytes 12582912 | tf_op jit(solution)/shard_map/dot_general | solution.py:65
  113.1 2.9 %copy.17 = f32[1024,512]{0,1:T(8,128)} copy(f32[1024,512]{1,0:T(8,128)} %add_add_fusion) | data formatting | bytes 4194304
  116.0 4.3 %multiply_reduce_fusion = f32[1024,4]{0,1:T(4,128)S(1)} fusion(f32[1024,512]{0,1:T(8,128)} %copy.17, bf16[4,512,1024]{2,1,0:T(8,128)(2,1)} %param.7, bf16[512,1024]{1,0:T(8,128)(2,1)S(1)} %bitcast.72), kind=kLoop, calls=%fused_computation | loop fusion | flops 8384512 | bytes 7356416 | tf_op jit(solution)/shard_map/cmg,mg->cg/dot_general | solution.py:69
  120.3 31.1 %all-gather.1 = f32[8,4,1024]{2,1,0:T(4,128)S(1)} all-gather(f32[1,4,1024]{2,1,0:T(4,128)S(1)} %bitcast.79), channel_id=2, replica_groups=mesh['row'=8,'col'=4] {'row'}, dimensions={0}, use_global_device_ids=true | all-gather | bytes 147456 | tf_op jit(solution)/shard_map/all_gather | solution.py:70
  151.5 0.0 copy-done.8
  151.5 0.0 copy-done.9
  151.5 0.1 multiply_multiply_fusion
  151.6 3.9 %fusion = f32[512,1024]{1,0:T(8,128)S(1)} fusion(f32[4,512,1024]{2,1,0:T(8,128)} %multiply_convert_fusion, f32[3,1024]{1,0:T(4,128)S(1)} %slice_multiply_fusion.2), kind=kLoop, calls=%fused_computation.2 | loop fusion | flops 2621440 | bytes 8400896 | tf_op jit(solution)/shard_map/reduce_sum | solution.py:88
  155.5 1.9 fusion.2
  157.4 1.9 fusion.5
  159.3 0.0 copy-start.5
  159.3 0.8 fusion.17
  160.1 1.7 fusion.4
  161.8 0.0 copy-done.5
  161.8 1.7 convolution_dynamic-update-slice_fusion.3
  163.6 1.7 convolution_dynamic-update-slice_fusion.2
  165.3 0.0 copy-done.3
  165.3 1.7 convolution_dynamic-update-slice_fusion.1
  167.0 0.0 copy-done.7
  167.0 1.7 convolution_dynamic-update-slice_fusion
  168.8 0.0 reduce-scatter.2.cloned.1.call-update
  168.8 52.7 %reduce-scatter.2.cloned.1.call-done = f32[128,2560]{0,1:T(8,128)} async-done(((f32[512,2560]{0,1:T(8,128)}), f32[128,2560]{0,1:T(8,128)}) %reduce-scatter.2.cloned.1.call-update) | async-done | bytes 1310736 | tf_op jit(solution)/shard_map/reduce_scatter | solution.py:96
  221.4 1.4 convert.4
  222.9 4.3 %collective-permute-start.4 = (bf16[128,512]{0,1:T(8,128)(2,1)S(1)}, bf16[128,512]{0,1:T(8,128)(2,1)S(1)}, u32[]{:S(2)}, u32[]{:S(2)}) collective-permute-start(bf16[128,512]{0,1:T(8,128)(2,1)S(1)} %get-tuple-element.8), channel_id=1, source_target_pairs={{4,0},{8,4},{12,8},{16,12},{20,16},{24,20},{28,24},{0,28},{5,1},{9... | collective-permute-start | bytes 393224 | tf_op jit(solution)/shard_map/ppermute | solution.py:16
  227.2 0.5 collective-permute-start.5
  227.7 3.4 %collective-permute-done.4 = bf16[128,512]{0,1:T(8,128)(2,1)S(1)} collective-permute-done((bf16[128,512]{0,1:T(8,128)(2,1)S(1)}, bf16[128,512]{0,1:T(8,128)(2,1)S(1)}, u32[]{:S(2)}, u32[]{:S(2)}) %collective-permute-start.4) | collective-permute-done | bytes 131104 | tf_op jit(solution)/shard_map/ppermute | solution.py:16
  231.0 1.5 collective-permute-done.5
  232.6 1.2 fusion.18
  233.7 0.1 pad_maximum_fusion
  233.8 1.1 copy.9
  (13 shorter events, 0.1 us)
Async XLA Ops:
  6.5 60.4 %copy-start = (f32[64]{0:T(128)S(1)}, f32[64]{0:T(128)}, u32[]{:S(2)}) copy-start(f32[64]{0:T(128)} %param.11) | copy-start | bytes 772
  6.5 214.9 %reduce-scatter.2.cloned.1.call-start = ((), (), s32[]{:S(2)}) async-start(), calls=%async_computation.1 | async-start | bytes 6553600 | tf_op jit(solution)/shard_map/reduce_scatter | solution.py:96
  10.5 7.1 %copy-start.1 = (bf16[4,512,1024]{2,1,0:T(8,128)(2,1)S(1)}, bf16[4,512,1024]{2,1,0:T(8,128)(2,1)}, u32[]{:S(2)}) copy-start(bf16[4,512,1024]{2,1,0:T(8,128)(2,1)} %param.7) | copy-start | bytes 12582916
  10.9 47.9 %collective-permute-start = (bf16[512,1024]{1,0:T(8,128)(2,1)S(1)}, bf16[512,1024]{1,0:T(8,128)(2,1)S(1)}, u32[]{:S(2)}, u32[]{:S(2)}) collective-permute-start(bf16[512,1024]{1,0:T(8,128)(2,1)S(1)} %bitcast.77), channel_id=1, source_target_pairs={{28,0},{0,4},{4,8},{8,12},{12,16},{16,20},{20,24},{24,28},{29,1},{... | collective-permute-start | bytes 3145736 | tf_op jit(solution)/shard_map/ppermute | solution.py:16
  14.0 49.6 %collective-permute-start.2 = (bf16[512,1024]{1,0:T(8,128)(2,1)S(1)}, bf16[512,1024]{1,0:T(8,128)(2,1)S(1)}, u32[]{:S(2)}, u32[]{:S(2)}) collective-permute-start(bf16[512,1024]{1,0:T(8,128)(2,1)S(1)} %bitcast.78), channel_id=1, source_target_pairs={{4,0},{8,4},{12,8},{16,12},{20,16},{24,20},{28,24},{0,28},{5,1},{9... | collective-permute-start | bytes 3145736 | tf_op jit(solution)/shard_map/ppermute | solution.py:16
  17.3 44.1 %slice-start = ((s8[5242880]{0:T(1024)(128)(4,1)}), s8[4194304]{0:T(1024)(128)(4,1)S(1)}, s32[]{:S(2)}) async-start(s8[5242880]{0:T(1024)(128)(4,1)} %bitcast.74), calls=%async_computation.2 | async-start | bytes 8388608
  17.6 43.8 %slice-start.1 = ((s8[5242880]{0:T(1024)(128)(4,1)}), s8[1048576]{0:T(1024)(128)(4,1)S(1)}, s32[]{:S(2)}) async-start(s8[5242880]{0:T(1024)(128)(4,1)} %bitcast.74), calls=%async_computation.3 | async-start | bytes 2097152
  21.8 45.1 %copy-start.10 = (s32[8]{0:T(128)S(1)}, s32[8]{0:T(128)}, u32[]{:S(2)}) copy-start(s32[8]{0:T(128)} %param.10) | copy-start | bytes 100
  58.9 10.4 %copy-start.2 = (bf16[512,1024]{1,0:T(8,128)(2,1)}, bf16[512,1024]{1,0:T(8,128)(2,1)S(1)}, u32[]{:S(2)}) copy-start(bf16[512,1024]{1,0:T(8,128)(2,1)S(1)} %collective-permute-done) | copy-start | bytes 3145732
  58.9 46.5 %collective-permute-start.1 = (bf16[512,1024]{1,0:T(8,128)(2,1)S(1)}, bf16[512,1024]{1,0:T(8,128)(2,1)S(1)}, u32[]{:S(2)}, u32[]{:S(2)}) collective-permute-start(bf16[512,1024]{1,0:T(8,128)(2,1)S(1)} %collective-permute-done), channel_id=1, source_target_pairs={{28,0},{0,4},{4,8},{8,12},{12,16},{16,20},{20,24},{24,28},{29,1},{... | collective-permute-start | bytes 3145736 | tf_op jit(solution)/shard_map/ppermute | solution.py:16
  63.6 7.9 %copy-start.4 = (bf16[512,1024]{1,0:T(8,128)(2,1)}, bf16[512,1024]{1,0:T(8,128)(2,1)S(1)}, u32[]{:S(2)}) copy-start(bf16[512,1024]{1,0:T(8,128)(2,1)S(1)} %collective-permute-done.2) | copy-start | bytes 3145732
  63.6 45.6 %collective-permute-start.3 = (bf16[512,1024]{1,0:T(8,128)(2,1)S(1)}, bf16[512,1024]{1,0:T(8,128)(2,1)S(1)}, u32[]{:S(2)}, u32[]{:S(2)}) collective-permute-start(bf16[512,1024]{1,0:T(8,128)(2,1)S(1)} %collective-permute-done.2), channel_id=1, source_target_pairs={{4,0},{8,4},{12,8},{16,12},{20,16},{24,20},{28,24},{0,28},{5,1},{9... | collective-permute-start | bytes 3145736 | tf_op jit(solution)/shard_map/ppermute | solution.py:16
  105.4 1.1 copy-start.6
  116.0 35.5 %copy-start.8 = (f32[1024]{0:T(1024)S(1)}, f32[1024]{0:T(1024)}, u32[]{:S(2)}) copy-start(f32[1024]{0:T(1024)} %param.12) | copy-start | bytes 12292
  116.0 35.5 %copy-start.9 = (f32[1024]{0:T(1024)S(1)}, f32[1024]{0:T(1024)}, u32[]{:S(2)}) copy-start(f32[1024]{0:T(1024)} %param.13) | copy-start | bytes 12292
  159.3 2.5 %copy-start.5 = (bf16[512,1024]{1,0:T(8,128)(2,1)S(1)}, bf16[512,1024]{1,0:T(8,128)(2,1)}, u32[]{:S(2)}) copy-start(bf16[512,1024]{1,0:T(8,128)(2,1)} %copy-done.4) | copy-start | bytes 3145732
  161.8 3.5 %copy-start.3 = (bf16[512,1024]{1,0:T(8,128)(2,1)S(1)}, bf16[512,1024]{1,0:T(8,128)(2,1)}, u32[]{:S(2)}) copy-start(bf16[512,1024]{1,0:T(8,128)(2,1)} %copy-done.2) | copy-start | bytes 3145732
  163.6 3.5 %copy-start.7 = (bf16[512,1024]{1,0:T(8,128)(2,1)S(1)}, bf16[512,1024]{1,0:T(8,128)(2,1)}, u32[]{:S(2)}) copy-start(bf16[512,1024]{1,0:T(8,128)(2,1)} %copy-done.6) | copy-start | bytes 3145732
  222.9 8.2 %collective-permute-start.4 = (bf16[128,512]{0,1:T(8,128)(2,1)S(1)}, bf16[128,512]{0,1:T(8,128)(2,1)S(1)}, u32[]{:S(2)}, u32[]{:S(2)}) collective-permute-start(bf16[128,512]{0,1:T(8,128)(2,1)S(1)} %get-tuple-element.8), channel_id=1, source_target_pairs={{4,0},{8,4},{12,8},{16,12},{20,16},{24,20},{28,24},{0,28},{5,1},{9... | collective-permute-start | bytes 393224 | tf_op jit(solution)/shard_map/ppermute | solution.py:16
  227.2 5.4 %collective-permute-start.5 = (bf16[128,512]{0,1:T(8,128)(2,1)S(1)}, bf16[128,512]{0,1:T(8,128)(2,1)S(1)}, u32[]{:S(2)}, u32[]{:S(2)}) collective-permute-start(bf16[128,512]{0,1:T(8,128)(2,1)S(1)} %get-tuple-element.9), channel_id=1, source_target_pairs={{8,0},{12,4},{16,8},{20,12},{24,16},{28,20},{0,24},{4,28},{9,1},{1... | collective-permute-start | bytes 393224 | tf_op jit(solution)/shard_map/ppermute | solution.py:16
Sparse Core Ops, SparseCore 0:
  168.9 52.4 reduce-scatter.1
